TPU v7x, 32 devices: a whole 2x2x4 slice. The times are simulated.
32 devices in a mesh: dp: 16 (over z, y, core), tensor: 2 (over x).
Axes of the slice: x: 2, y: 2, z: 4, core: 2. Of those that a mesh axis runs over, the one named last changes fastest.
Arguments:
- tokens: bfloat16 [32, 512, 768], P('dp', 'tensor')
- prob_masks: int32 [2, 32, 12, 512, 40], P(None, 'dp', 'tensor'), may hold values from 0 to 8191, as said below
- branch_masks: int32 [2, 2, 32, 512, 52], P(None, None, 'dp', 'tensor'), may hold values from 0 to 32767, as said below
- attn_weight: float32 [768, 3, 768], P('dp', None, 'tensor'), may hold values from -0.21875 to 0.21875
- attn_first: float32 [768, 3, 768], P('dp', None, 'tensor'), may hold values from -3.0517578e-05 to 3.0517578e-05
- attn_second: float32 [768, 3, 768], P('dp', None, 'tensor'), may hold values from 1.159668e-12 to 1.8615722e-11
- out_weight: float32 [768, 768], P('tensor', 'dp'), may hold values from -0.4375 to 0.4375
- out_first: float32 [768, 768], P('tensor', 'dp'), may hold values from -3.0517578e-05 to 3.0517578e-05
- out_second: float32 [768, 768], P('tensor', 'dp'), may hold values from 1.159668e-12 to 1.8615722e-11
- up_weight: float32 [768, 3072], P('dp', 'tensor'), may hold values from -0.21875 to 0.21875
- up_first: float32 [768, 3072], P('dp', 'tensor'), may hold values from -3.0517578e-05 to 3.0517578e-05
- up_second: float32 [768, 3072], P('dp', 'tensor'), may hold values from 1.159668e-12 to 1.8615722e-11
- down_weight: float32 [3072, 768], P('tensor', 'dp'), may hold values from -0.109375 to 0.109375
- down_first: float32 [3072, 768], P('tensor', 'dp'), may hold values from -3.0517578e-05 to 3.0517578e-05
- down_second: float32 [3072, 768], P('tensor', 'dp'), may hold values from 1.159668e-12 to 1.8615722e-11
- gains: float32 [2, 768], replicated, may hold values from 0.5 to 1.5
- gains_first: float32 [2, 768], replicated, may hold values from -0.00012207031 to 0.00012207031
- gains_second: float32 [2, 768], replicated, may hold values from 1.8615722e-11 to 2.9907227e-10
- shifts: float32 [6, 768], replicated, may hold values from -1.25 to 1.25
- shifts_first: float32 [6, 768], replicated, may hold values from -0.00012207031 to 0.00012207031
- shifts_second: float32 [6, 768], replicated, may hold values from 1.8615722e-11 to 2.9907227e-10
- hidden_bias: float32 [3072], replicated, may hold values from -1.25 to 1.25
- hidden_first: float32 [3072], replicated, may hold values from -0.00012207031 to 0.00012207031
- hidden_second: float32 [3072], replicated, may hold values from 1.8615722e-11 to 2.9907227e-10
Outputs:
- loss: float32 [], replicated
- grad_tokens: float32 [32, 512, 768], P('dp', 'tensor')
- new_attn: float32 [768, 3, 768], P('dp', None, 'tensor')
- new_attn_first: float32 [768, 3, 768], P('dp', None, 'tensor')
- new_attn_second: float32 [768, 3, 768], P('dp', None, 'tensor')
- new_out: float32 [768, 768], P('tensor', 'dp')
- new_out_first: float32 [768, 768], P('tensor', 'dp')
- new_out_second: float32 [768, 768], P('tensor', 'dp')
- new_up: float32 [768, 3072], P('dp', 'tensor')
- new_up_first: float32 [768, 3072], P('dp', 'tensor')
- new_up_second: float32 [768, 3072], P('dp', 'tensor')
- new_down: float32 [3072, 768], P('tensor', 'dp')
- new_down_first: float32 [3072, 768], P('tensor', 'dp')
- new_down_second: float32 [3072, 768], P('tensor', 'dp')
- new_gains: float32 [2, 768], replicated
- new_gains_first: float32 [2, 768], replicated
- new_gains_second: float32 [2, 768], replicated
- new_shifts: float32 [6, 768], replicated
- new_shifts_first: float32 [6, 768], replicated
- new_shifts_second: float32 [6, 768], replicated
- new_hidden: float32 [3072], replicated
- new_hidden_first: float32 [3072], replicated
- new_hidden_second: float32 [3072], replicated
Inputs may be any that keep to these rules, and one draw needn't show every extreme that they name: `prob_masks`: each word holds 13 keep bits for 13 consecutive keys, bit b of word w for key 13 w + b; bits for keys at 512 or past are zero. `branch_masks`: each word holds 15 keep bits for 15 consecutive features, bit b of word w for feature 15 w + b; bits for features at 768 or past are zero.
All inputs are finite; a program needn't handle non-finite values.
Results may differ from a plain program's by a relative error of at most 0.009.
Values may be sent and summed in bfloat16 or wider, within the bound.
No kernel may reach another device: no remote copies, remote signals or barrier semaphores. Data moves between devices by JAX's collectives and lax.ppermute only.
A program may use at most 192 MiB of HBM per device.

v0:
```python
import jax
import jax.numpy as jnp
from jax import lax
from jax.sharding import PartitionSpec as P

HD = 64
STEP = 10
KEEP_SCALE = 1.0 / 0.9


def unpack(packed, length, word_bits):
    places = jnp.arange(word_bits, dtype=jnp.int32)
    bit_flags = jnp.bitwise_and(jnp.right_shift(packed[..., None], places), 1)
    bit_flags = bit_flags.reshape(packed.shape[:-1] + (packed.shape[-1] * word_bits,))
    return bit_flags[..., :length].astype(jnp.float32) * KEEP_SCALE


def layer_norm(values_in, gain_row, shift_row):
    center = values_in - jnp.mean(values_in, axis=-1, keepdims=True)
    spread = jnp.mean(center * center, axis=-1, keepdims=True)
    return center * lax.rsqrt(spread + 1e-12) * gain_row + shift_row


def contrastive(pooled):
    unit_rows = pooled * lax.rsqrt(jnp.sum(pooled * pooled, axis=-1, keepdims=True) + 1e-06)
    logits = jnp.dot(unit_rows[0], unit_rows[1].T, precision=lax.Precision.HIGHEST) * 20.0
    return jnp.mean(jax.nn.logsumexp(logits, axis=1) - jnp.diagonal(logits))


def gelu_exact(values_in):
    return jax.nn.gelu(values_in, approximate=False)


def contract(left_side, right_side, left_dim, right_dim):
    return lax.dot_general(
        left_side,
        right_side,
        (((left_dim,), (right_dim,)), ((), ())),
        preferred_element_type=jnp.float32,
    )


def attend_forward(queries, key_rows, values, prob_words):
    length = queries.shape[0]
    scores = (
        jnp.einsum("qhd,khd->hqk", queries, key_rows, preferred_element_type=jnp.float32) * 0.125
    )
    row_peak = jnp.max(scores, axis=-1, keepdims=True)
    sum_exp = jnp.sum(jnp.exp(scores - row_peak), axis=-1, keepdims=True)
    logsum = row_peak + jnp.log(sum_exp)
    attn_probs = jnp.exp(scores - logsum)
    weighted = (attn_probs[None] * unpack(prob_words, length, 13)).astype(jnp.bfloat16)
    context = jnp.einsum("vhqk,khd->vqhd", weighted, values, preferred_element_type=jnp.float32)
    return (context.astype(jnp.bfloat16).reshape(2, length, -1), logsum[..., 0])


def attend_backward(queries, key_rows, values, prob_words, logsum, grad_context):
    length = queries.shape[0]
    scores = (
        jnp.einsum("qhd,khd->hqk", queries, key_rows, preferred_element_type=jnp.float32) * 0.125
    )
    attn_probs = jnp.exp(scores - logsum[..., None])
    keep_probs = unpack(prob_words, length, 13)
    weighted = (attn_probs[None] * keep_probs).astype(jnp.bfloat16)
    grad_values = jnp.einsum(
        "vhqk,vqhd->khd", weighted, grad_context, preferred_element_type=jnp.float32
    )
    grad_weighted = jnp.einsum(
        "vqhd,khd->vhqk", grad_context, values, preferred_element_type=jnp.float32
    )
    grad_probs = jnp.sum(grad_weighted * keep_probs, axis=0)
    inner = jnp.sum(grad_probs * attn_probs, axis=-1, keepdims=True)
    grad_scores = (attn_probs * (grad_probs - inner)).astype(jnp.bfloat16)
    grad_queries = (
        jnp.einsum("hqk,khd->qhd", grad_scores, key_rows, preferred_element_type=jnp.float32)
        * 0.125
    )
    grad_keys = (
        jnp.einsum("hqk,qhd->khd", grad_scores, queries, preferred_element_type=jnp.float32) * 0.125
    )
    return jnp.stack([grad_queries, grad_keys, grad_values], axis=1)


def adam_direction(weight, gradient, first_moment, second, decay_rate):
    new_first = 0.9 * first_moment + 0.1 * gradient
    new_second = 0.999 * second + 0.001 * gradient * gradient
    first_hat = new_first / (1.0 - 0.9**STEP)
    second_hat = new_second / (1.0 - 0.999**STEP)
    update = first_hat / (jnp.sqrt(second_hat) + 1e-06) + decay_rate * weight
    return (new_first, new_second, update)


def small_step(weight, gradient, first_moment, second):
    new_first, new_second, update = adam_direction(weight, gradient, first_moment, second, 0.0)
    trust_ratio = jnp.sqrt(jnp.sum(weight * weight, axis=-1, keepdims=True)) / jnp.sqrt(
        jnp.sum(update * update, axis=-1, keepdims=True)
    )
    return (weight - 0.25 * trust_ratio * update, new_first, new_second)


def shards(
    tokens,
    prob_masks,
    branch_masks,
    attn_weight,
    attn_first,
    attn_second,
    out_weight,
    out_first,
    out_second,
    up_weight,
    up_first,
    up_second,
    down_weight,
    down_first,
    down_second,
    gains,
    gains_first,
    gains_second,
    shifts,
    shifts_first,
    shifts_second,
    hidden_bias,
    hidden_first,
    hidden_second,
):
    tensor_count = lax.axis_size("tensor")
    tensor_rank = lax.axis_index("tensor")
    data_count = lax.axis_size("dp")
    data_rank = lax.axis_index("dp")
    seq_local, half_len, model_width = tokens.shape
    seq_len = half_len * tensor_count
    heads_local = prob_masks.shape[2]
    local_width = heads_local * HD
    hidden_local = up_weight.shape[1]
    scale_loss = 64.0 * data_count * seq_local * seq_len
    attn_low, out_low, up_low, down_low = (
        lax.all_gather(attn_weight.astype(jnp.bfloat16), "dp", axis=0, tiled=True),
        lax.all_gather(out_weight.astype(jnp.bfloat16), "dp", axis=1, tiled=True),
        lax.all_gather(up_weight.astype(jnp.bfloat16), "dp", axis=0, tiled=True),
        lax.all_gather(down_weight.astype(jnp.bfloat16), "dp", axis=1, tiled=True),
    )
    token_full = lax.all_gather(tokens, "tensor", axis=1, tiled=True)
    token_flat = token_full.reshape(seq_local * seq_len, model_width)
    attn_matrix = attn_low.reshape(model_width, 3 * local_width)
    bias_query = lax.dynamic_slice_in_dim(shifts[0], tensor_rank * local_width, local_width)
    bias_value = lax.dynamic_slice_in_dim(shifts[1], tensor_rank * local_width, local_width)
    qkv_bias = jnp.stack([bias_query, jnp.zeros_like(bias_query), bias_value])
    projected = (
        jnp.dot(token_flat, attn_matrix, preferred_element_type=jnp.float32).reshape(
            seq_local, seq_len, 3, local_width
        )
        + qkv_bias
    )
    qkv_low = projected.astype(jnp.bfloat16)
    heads_shape = (seq_local, seq_len, heads_local, HD)
    queries = qkv_low[:, :, 0].reshape(heads_shape)
    key_rows = qkv_low[:, :, 1].reshape(heads_shape)
    values = qkv_low[:, :, 2].reshape(heads_shape)
    mask_words = jnp.moveaxis(prob_masks, 1, 0)
    context, logsum = lax.map(
        lambda sequence_items: attend_forward(*sequence_items),
        (queries, key_rows, values, mask_words),
    )
    context_flat = jnp.moveaxis(context, 1, 0).reshape(-1, local_width)
    attn_part = jnp.dot(context_flat, out_low, preferred_element_type=jnp.float32).reshape(
        2, seq_local, seq_len, model_width
    )
    attn_out = (
        lax.psum_scatter(
            attn_part.astype(jnp.bfloat16), "tensor", scatter_dimension=2, tiled=True
        ).astype(jnp.float32)
        + shifts[2]
    )
    keep_attn = unpack(branch_masks[0], model_width, 15)
    keep_ffn = unpack(branch_masks[1], model_width, 15)
    first_in = tokens.astype(jnp.float32)[None] + attn_out * keep_attn
    normed, norm_one_back = jax.vjp(layer_norm, first_in, gains[0], shifts[3])
    normed_full = lax.all_gather(normed.astype(jnp.bfloat16), "tensor", axis=2, tiled=True)
    normed_flat = normed_full.reshape(-1, model_width)
    bias_hidden = lax.dynamic_slice_in_dim(hidden_bias, tensor_rank * hidden_local, hidden_local)
    hidden_pre = jnp.dot(normed_flat, up_low, preferred_element_type=jnp.float32) + bias_hidden
    gelu_value, gelu_back = jax.vjp(gelu_exact, hidden_pre)
    active = gelu_value.astype(jnp.bfloat16)
    ffn_part = jnp.dot(active, down_low, preferred_element_type=jnp.float32).reshape(
        2, seq_local, seq_len, model_width
    )
    ffn_out = (
        lax.psum_scatter(
            ffn_part.astype(jnp.bfloat16), "tensor", scatter_dimension=2, tiled=True
        ).astype(jnp.float32)
        + shifts[4]
    )
    output, norm_two_back = jax.vjp(layer_norm, normed + ffn_out * keep_ffn, gains[1], shifts[5])
    pooled_part = jnp.sum(output, axis=2) / seq_len
    pooled_all = lax.all_gather(pooled_part, ("dp", "tensor"), axis=1, tiled=True)
    pooled = (
        pooled_all.reshape(2, data_count, tensor_count, seq_local, model_width)
        .sum(axis=2)
        .reshape(2, data_count * seq_local, model_width)
    )
    loss_value, loss_back = jax.vjp(contrastive, pooled)
    grad_pooled = loss_back(jnp.float32(scale_loss))[0]
    grad_own = lax.dynamic_slice_in_dim(grad_pooled, data_rank * seq_local, seq_local, axis=1)
    grad_output = jnp.broadcast_to((grad_own / seq_len)[:, :, None, :], output.shape)
    grad_second, grad_gain_two, grad_shift_two = norm_two_back(grad_output)
    grad_ffn = (grad_second * keep_ffn).astype(jnp.bfloat16)
    grad_ffn_full = lax.all_gather(grad_ffn, "tensor", axis=2, tiled=True)
    grad_ffn_flat = grad_ffn_full.reshape(-1, model_width)
    grad_down = contract(active, grad_ffn_flat, 0, 0)
    grad_active = contract(grad_ffn_flat, down_low, 1, 1)
    grad_hidden = gelu_back(grad_active)[0].astype(jnp.bfloat16)
    grad_up = contract(normed_flat, grad_hidden, 0, 0)
    normed_back = contract(grad_hidden, up_low, 1, 1).reshape(2, seq_local, seq_len, model_width)
    grad_normed = grad_second + lax.psum_scatter(
        normed_back.astype(jnp.bfloat16), "tensor", scatter_dimension=2, tiled=True
    ).astype(jnp.float32)
    grad_first, grad_gain_one, grad_shift_one = norm_one_back(grad_normed)
    grad_attn = (grad_first * keep_attn).astype(jnp.bfloat16)
    grad_attn_full = lax.all_gather(grad_attn, "tensor", axis=2, tiled=True)
    grad_attn_flat = grad_attn_full.reshape(-1, model_width)
    grad_out = contract(context_flat, grad_attn_flat, 0, 0)
    grad_context = (
        contract(grad_attn_flat, out_low, 1, 1)
        .astype(jnp.bfloat16)
        .reshape(2, seq_local, seq_len, heads_local, HD)
    )
    grad_qkv = lax.map(
        lambda sequence_items: attend_backward(*sequence_items),
        (queries, key_rows, values, mask_words, logsum, jnp.moveaxis(grad_context, 1, 0)),
    )
    qkv_grad_low = grad_qkv.reshape(seq_local * seq_len, 3 * local_width).astype(jnp.bfloat16)
    grad_attn_weight = contract(token_flat, qkv_grad_low, 0, 0).reshape(model_width, 3, local_width)
    attn_reduced, out_reduced, up_reduced, down_reduced = (
        lax.psum_scatter(grad_attn_weight, "dp", scatter_dimension=0, tiled=True),
        lax.psum_scatter(grad_out, "dp", scatter_dimension=1, tiled=True),
        lax.psum_scatter(grad_up, "dp", scatter_dimension=0, tiled=True),
        lax.psum_scatter(grad_down, "dp", scatter_dimension=1, tiled=True),
    )
    token_back = contract(qkv_grad_low, attn_matrix, 1, 1).reshape(seq_local, seq_len, model_width)
    grad_tokens = lax.psum_scatter(
        token_back.astype(jnp.bfloat16), "tensor", scatter_dimension=1, tiled=True
    ).astype(jnp.float32) + jnp.sum(grad_first, axis=0)
    qkv_sums = jnp.sum(qkv_grad_low.astype(jnp.float32).reshape(-1, 3, local_width), axis=0)
    zero_row = jnp.zeros((model_width,), jnp.float32)
    query_row = lax.dynamic_update_slice_in_dim(zero_row, qkv_sums[0], tensor_rank * local_width, 0)
    value_row = lax.dynamic_update_slice_in_dim(zero_row, qkv_sums[2], tensor_rank * local_width, 0)
    shift_grads = jnp.stack(
        [
            query_row,
            value_row,
            jnp.sum(grad_attn.astype(jnp.float32), axis=(0, 1, 2)),
            grad_shift_one,
            jnp.sum(grad_ffn.astype(jnp.float32), axis=(0, 1, 2)),
            grad_shift_two,
        ]
    )
    gain_grads = jnp.stack([grad_gain_one, grad_gain_two])
    hidden_grads = lax.dynamic_update_slice_in_dim(
        jnp.zeros((hidden_local * tensor_count,), jnp.float32),
        jnp.sum(grad_hidden.astype(jnp.float32), axis=0),
        tensor_rank * hidden_local,
        0,
    )
    attn_new_first, attn_new_second, attn_update = adam_direction(
        attn_weight, attn_reduced / scale_loss, attn_first, attn_second, 0.01
    )
    out_new_first, out_new_second, out_update = adam_direction(
        out_weight, out_reduced / scale_loss, out_first, out_second, 0.01
    )
    up_new_first, up_new_second, up_update = adam_direction(
        up_weight, up_reduced / scale_loss, up_first, up_second, 0.01
    )
    down_new_first, down_new_second, down_update = adam_direction(
        down_weight, down_reduced / scale_loss, down_first, down_second, 0.01
    )
    squares = jnp.concatenate(
        [
            jnp.sum(attn_weight * attn_weight, axis=(0, 2)),
            jnp.stack(
                [
                    jnp.sum(out_weight * out_weight),
                    jnp.sum(up_weight * up_weight),
                    jnp.sum(down_weight * down_weight),
                ]
            ),
            jnp.sum(attn_update * attn_update, axis=(0, 2)),
            jnp.stack(
                [
                    jnp.sum(out_update * out_update),
                    jnp.sum(up_update * up_update),
                    jnp.sum(down_update * down_update),
                ]
            ),
        ]
    )
    summed_squares, gain_total, shift_total, hidden_total = lax.psum(
        (squares, gain_grads, shift_grads, hidden_grads), ("dp", "tensor")
    )
    trust_ratio = jnp.sqrt(summed_squares[:6]) / jnp.sqrt(summed_squares[6:])
    new_attn = attn_weight - 0.25 * trust_ratio[0:3][None, :, None] * attn_update
    new_out = out_weight - 0.25 * trust_ratio[3] * out_update
    new_up = up_weight - 0.25 * trust_ratio[4] * up_update
    new_down = down_weight - 0.25 * trust_ratio[5] * down_update
    new_gains, new_gains_first, new_gains_second = small_step(
        gains, gain_total / scale_loss, gains_first, gains_second
    )
    new_shifts, new_shifts_first, new_shifts_second = small_step(
        shifts, shift_total / scale_loss, shifts_first, shifts_second
    )
    new_hidden, new_hidden_first, new_hidden_second = small_step(
        hidden_bias, hidden_total / scale_loss, hidden_first, hidden_second
    )
    return (
        loss_value,
        grad_tokens,
        new_attn,
        attn_new_first,
        attn_new_second,
        new_out,
        out_new_first,
        out_new_second,
        new_up,
        up_new_first,
        up_new_second,
        new_down,
        down_new_first,
        down_new_second,
        new_gains,
        new_gains_first,
        new_gains_second,
        new_shifts,
        new_shifts_first,
        new_shifts_second,
        new_hidden,
        new_hidden_first,
        new_hidden_second,
    )


def solution(mesh):
    return jax.shard_map(
        shards,
        mesh=mesh,
        in_specs=(
            P("dp", "tensor", None),
            P(None, "dp", "tensor", None, None),
            P(None, None, "dp", "tensor", None),
            P("dp", None, "tensor"),
            P("dp", None, "tensor"),
            P("dp", None, "tensor"),
            P("tensor", "dp"),
            P("tensor", "dp"),
            P("tensor", "dp"),
            P("dp", "tensor"),
            P("dp", "tensor"),
            P("dp", "tensor"),
            P("tensor", "dp"),
            P("tensor", "dp"),
            P("tensor", "dp"),
            P(),
            P(),
            P(),
            P(),
            P(),
            P(),
            P(),
            P(),
            P(),
        ),
        out_specs=(
            P(),
            P("dp", "tensor", None),
            P("dp", None, "tensor"),
            P("dp", None, "tensor"),
            P("dp", None, "tensor"),
            P("tensor", "dp"),
            P("tensor", "dp"),
            P("tensor", "dp"),
            P("dp", "tensor"),
            P("dp", "tensor"),
            P("dp", "tensor"),
            P("tensor", "dp"),
            P("tensor", "dp"),
            P("tensor", "dp"),
            P(),
            P(),
            P(),
            P(),
            P(),
            P(),
            P(),
            P(),
            P(),
        ),
        check_vma=False,
    )
```

profile of v0, /device:TPU:0, one launch (start us, length us, event | category | flops | bytes accessed | tf_op | source)
XLA Modules:
  0.0 1080.3 jit_solution(10038383568165098798)
XLA Ops:
  14.4 27.1 %all_gather.29 = bf16[384,768]{0,1:T(8,128)(2,1)} all-gather(bf16[384,48]{0,1:T(8,128)(2,1)S(1)} %convert_element_type.122), channel_id=1, replica_groups=mesh['dp'=16,'tensor'=2] {'dp'}, dimensions={1}, use_global_device_ids=true | all-gather | bytes 626688 | tf_op jit(solution)/shard_map/all_gather | solution.py:139
  41.6 13.7 %all-gather.10.cloned.1.call-done = bf16[768,3,384]{2,0,1:T(8,128)(2,1)} async-done(((bf16[48,3,384]{2,0,1:T(8,128)(2,1)}), bf16[768,3,384]{2,0,1:T(8,128)(2,1)}) %all-gather.10.cloned.1.call-update) | async-done | bytes 1769488 | tf_op jit(solution)/shard_map/all_gather | solution.py:138
  55.3 3.9 copy.163
  59.1 23.8 %all-gather.8.cloned.1.call-done = bf16[2,512,768]{2,1,0:T(8,128)(2,1)} async-done(((bf16[2,256,768]{2,1,0:T(8,128)(2,1)}), bf16[2,512,768]{2,1,0:T(8,128)(2,1)}) %all-gather.8.cloned.1.call-update) | async-done | bytes 1572880 | tf_op jit(solution)/shard_map/all_gather | solution.py:143
  83.0 4.0 add_convert_fusion.1
  88.1 108.0 %while.22 = (s32[]{:T(128)}, bf16[2,2,512,384]{2,3,1,0:T(8,128)(2,1)}, f32[2,6,512]{2,1,0:T(8,128)}, bf16[2,512,6,64]{1,3,2,0:T(8,128)(2,1)}, s32[2,2,6,512,40]{...) while((s32[]{:T(128)}, ...), condition=%wide.region_3.4_spmd, body=%wide.region_0.3_spmd.sunk | while | flops 632681472 | bytes 140713456 | solution.py:161
  88.4 3.6 shift_right_arithmetic.162
  92.0 6.3 slice.162
  98.3 19.0 %copy.239 = s32[2,6,512,512]{3,2,1,0:T(8,128)} copy(s32[2,6,512,512]{2,0,3,1:T(2,128)} %slice.162) | data formatting | bytes 25165824 | tf_op jit(solution)/shard_map/while
  121.6 3.7 exponential_multiply_fusion.2
  125.2 6.6 copy.240
  131.9 8.9 fusion.134
  142.4 3.6 shift_right_arithmetic.162
  146.0 6.3 slice.162
  152.3 19.0 %copy.239 = s32[2,6,512,512]{3,2,1,0:T(8,128)} copy(s32[2,6,512,512]{2,0,3,1:T(2,128)} %slice.162) | data formatting | bytes 25165824 | tf_op jit(solution)/shard_map/while
  175.6 3.7 exponential_multiply_fusion.2
  179.2 6.6 copy.240
  185.8 8.9 fusion.134
  196.1 6.3 convolution_convert_fusion.3
  204.2 9.9 all-gather.12.cloned.1.call-start
  220.5 4.1 copy.202
  224.6 21.2 %reduce-scatter.9.cloned.1.call-done = bf16[2,2,256,768]{3,2,1,0:T(8,128)(2,1)} async-done(((bf16[2,2,512,768]{3,2,1,0:T(8,128)(2,1)}), bf16[2,2,256,768]{3,2,1,0:T(8,128)(2,1)}) %reduce-scatter.9.cloned.1.call-update) | async-done | bytes 1572880 | tf_op jit(solution)/shard_map/reduce_scatter | solution.py:170
  253.1 37.9 %all-gather.14.cloned.1.call-done = bf16[768,1536]{1,0:T(8,128)(2,1)} async-done(((bf16[48,1536]{1,0:T(8,128)(2,1)}), bf16[768,1536]{1,0:T(8,128)(2,1)}) %all-gather.14.cloned.1.call-update) | async-done | bytes 2359312 | tf_op jit(solution)/shard_map/all_gather | solution.py:140
  291.1 45.2 %all-gather.12.cloned.1.call-done = bf16[2,2,512,768]{3,2,1,0:T(8,128)(2,1)} async-done(((bf16[2,2,256,768]{3,2,1,0:T(8,128)(2,1)}), bf16[2,2,512,768]{3,2,1,0:T(8,128)(2,1)}) %all-gather.12.cloned.1.call-update) | async-done | bytes 3145744 | tf_op jit(solution)/shard_map/all_gather | solution.py:179
  336.3 34.9 %multiply_convert_fusion.6 = (bf16[2048,1536]{1,0:T(8,128)(2,1)}, f32[2048,1536]{1,0:T(8,128)}, f32[2048,1536]{1,0:T(8,128)}) fusion(f32[1536]{0:T(1024)S(1)} %dynamic_slice.48, bf16[2048,768]{1,0:T(8,128)(2,1)} %bitcast.269, bf16[768,1536]{1,0:T(8,128)(2,1)} %all-gather.14.cloned.1.call-done), kind=kOutput, calls=%fused_computation.68 | convolution fusion | flops 5039456256 | bytes 36968448 | tf_op jit(solution)/shard_map/dot_general | solution.py:182
  371.2 10.4 all-gather.16.cloned.1.call-done
  381.5 9.1 convolution_convert_fusion.1
  392.8 3.6 copy.203
  396.9 36.0 %reduce-scatter.11.cloned.1.call-done = bf16[2,2,256,768]{3,2,1,0:T(8,128)(2,1)} async-done(((bf16[2,2,512,768]{3,2,1,0:T(8,128)(2,1)}), bf16[2,2,256,768]{3,2,1,0:T(8,128)(2,1)}) %reduce-scatter.11.cloned.1.call-update) | async-done | bytes 1572880 | tf_op jit(solution)/shard_map/reduce_scatter | solution.py:189
  433.0 4.1 fusion.84
  438.9 74.0 %all_gather.33 = f32[2,64,768]{2,0,1:T(2,128)} all-gather(f32[2,2,768]{2,0,1:T(2,128)S(1)} %copy.168), channel_id=1, replica_groups=mesh['dp'=16,'tensor'=2] {'dp','tensor'}, dimensions={1}, use_global_device_ids=true | all-gather | bytes 405504 | tf_op jit(solution)/shard_map/all_gather | solution.py:196
  535.5 40.5 %all-gather.18.cloned.1.call-done = bf16[2,2,512,768]{3,2,1,0:T(8,128)(2,1)} async-done(((bf16[2,2,256,768]{3,2,1,0:T(8,128)(2,1)}), bf16[2,2,512,768]{3,2,1,0:T(8,128)(2,1)}) %all-gather.18.cloned.1.call-update) | async-done | bytes 3145744 | tf_op jit(solution)/shard_map/all_gather | solution.py:208
  576.1 17.6 %convert_reduce_fusion = (f32[1536]{0:T(1024)}, bf16[2048,1536]{1,0:T(8,128)(2,1)S(1)}) fusion(f32[2048,1536]{1,0:T(8,128)} %get-tuple-element.243, bf16[2048,768]{1,0:T(8,128)(2,1)} %bitcast.271, bf16[1536,768]{0,1:T(8,128)(2,1)} %all-gather.16.cloned.1.call-done, f32[2048,1536]{1,0:T(8,128)} %get-tuple-element.270, f32[1536]{0:T(1024)S(1)} %copy-done.87), kind=kOutput, calls=%fused_computation.66 | convolution fusion | flops 4885314048 | bytes 36974592 | tf_op jit(solution)/shard_map/dot_general | solution.py:35
  593.6 6.5 convolution_convert_fusion
  600.3 43.4 %reduce-scatter.13.cloned.1.call-done = bf16[2,2,256,768]{3,2,1,0:T(8,128)(2,1)} async-done(((bf16[2,2,512,768]{3,2,1,0:T(8,128)(2,1)}), bf16[2,2,256,768]{3,2,1,0:T(8,128)(2,1)}) %reduce-scatter.13.cloned.1.call-update) | async-done | bytes 1572880 | tf_op jit(solution)/shard_map/reduce_scatter | solution.py:215
  643.7 5.0 multiply_reduce_fusion.3
  651.3 3.3 convert_reduce_fusion.3
  654.7 9.6 fusion.92
  666.4 9.5 fusion.93
  676.1 23.6 %all-gather.20.cloned.1.call-done = bf16[2,2,512,768]{3,2,1,0:T(8,128)(2,1)} async-done(((bf16[2,2,256,768]{3,2,1,0:T(8,128)(2,1)}), bf16[2,2,512,768]{3,2,1,0:T(8,128)(2,1)}) %all-gather.20.cloned.1.call-update) | async-done | bytes 3145744 | tf_op jit(solution)/shard_map/all_gather | solution.py:220
  699.7 3.7 convolution_convert_fusion.2
  707.8 4.5 convolution_bitcast_fusion
  712.6 93.9 %while.23 = (s32[]{:T(128)}, bf16[2,512,3,6,64]{1,4,3,2,0:T(8,128)(2,1)}, bf16[2,512,6,64]{1,3,2,0:T(8,128)(2,1)S(1)}, bf16[2,512,6,64]{1,3,2,0:T(8,128)(2,1)}, ...) while((s32[]{:T(128)}, ...), condition=%wide.region_26.27_spmd, body=%wide.region_23.26_spmd.sunk | while | flops 1462367232 | bytes 228946432 | solution.py:228
  713.0 3.6 shift_right_arithmetic.169
  716.6 6.3 slice.164
  723.0 12.5 %fusion.142 = f32[6,512,512]{1,2,0:T(8,128)} fusion(s32[2,6,512,512]{2,0,3,1:T(2,128)} %slice.164, s32[512]{0:T(512)S(1)} %slice.165, bf16[2,2,512,6,64]{2,4,1,3,0:T(8,128)(2,1)} %get-tuple-element.435, s32[]{:T(128)S(6)} %copy.259, bf16[2,512,6,64]{1,3,2,0:T(8,128)(2,1)} %get-tuple-element.434), kind=kOutput, calls=%fused_computation.27.clone.1 | convolution fusion | flops 419954688 | bytes 20057088 | tf_op jit(solution)/shard_map/while/body/eval_jaxpr/vqhd,khd->vhqk/dot_general | solution.py:68
  735.6 4.8 multiply_reduce_fusion.25
  740.4 5.6 multiply_convert_fusion.18
  747.3 6.1 fusion.143
  759.4 3.6 shift_right_arithmetic.169
  763.0 6.3 slice.164
  769.4 12.4 %fusion.142 = f32[6,512,512]{1,2,0:T(8,128)} fusion(s32[2,6,512,512]{2,0,3,1:T(2,128)} %slice.164, s32[512]{0:T(512)S(1)} %slice.165, bf16[2,2,512,6,64]{2,4,1,3,0:T(8,128)(2,1)} %get-tuple-element.435, s32[]{:T(128)S(6)} %copy.259, bf16[2,512,6,64]{1,3,2,0:T(8,128)(2,1)} %get-tuple-element.434), kind=kOutput, calls=%fused_computation.27.clone.1 | convolution fusion | flops 419954688 | bytes 20057088 | tf_op jit(solution)/shard_map/while/body/eval_jaxpr/vqhd,khd->vhqk/dot_general | solution.py:68
  781.8 4.8 multiply_reduce_fusion.25
  786.7 5.9 multiply_convert_fusion.18
  793.9 6.3 fusion.143
  800.3 3.4 fusion.144
  806.5 4.1 copy.178
  818.7 5.0 convolution_convert_fusion.4
  829.9 28.2 %reduce-scatter.23.cloned.1.call-done = f32[1536,48]{0,1:T(8,128)} async-done(((f32[1536,768]{0,1:T(8,128)}), f32[1536,48]{0,1:T(8,128)}) %reduce-scatter.23.cloned.1.call-update) | async-done | bytes 294928 | tf_op jit(solution)/shard_map/reduce_scatter | solution.py:238
  862.3 56.9 %reduce-scatter.19.cloned.1.call-done = f32[384,48]{0,1:T(8,128)} async-done(((f32[384,768]{0,1:T(8,128)}), f32[384,48]{0,1:T(8,128)}) %reduce-scatter.19.cloned.1.call-update) | async-done | bytes 73744 | tf_op jit(solution)/shard_map/reduce_scatter | solution.py:236
  920.8 69.6 %reduce-scatter.17.cloned.1.call-done = f32[48,3,384]{2,0,1:T(8,128)} async-done(((f32[768,3,384]{2,0,1:T(8,128)}), f32[48,3,384]{2,0,1:T(8,128)}) %reduce-scatter.17.cloned.1.call-update) | async-done | bytes 221200 | tf_op jit(solution)/shard_map/reduce_scatter | solution.py:235
  991.9 4.0 concatenate.8
  995.9 22.3 %reduce-scatter.15.cloned.1.call-done = bf16[2,256,768]{2,1,0:T(8,128)(2,1)} async-done(((bf16[2,512,768]{2,1,0:T(8,128)(2,1)}), bf16[2,256,768]{2,1,0:T(8,128)(2,1)}) %reduce-scatter.15.cloned.1.call-update) | async-done | bytes 786448 | tf_op jit(solution)/shard_map/reduce_scatter | solution.py:241
  1021.1 40.1 %all-reduce.2 = (f32[12]{0:T(128)S(1)}, f32[2,768]{1,0:T(2,128)S(1)}, f32[6,768]{1,0:T(8,128)S(1)}, f32[3072]{0:T(1024)S(1)}) all-reduce(f32[12]{0:T(128)S(1)} %concatenate.8, f32[2,768]{1,0:T(2,128)S(1)} %copy-done.71, f32[6,768]{1,0:T(8,128)S(1)} %stack.81, ...), channel_id=1, replica_groups=mesh['dp'=16,'tensor'=2] {'dp','tensor'}, use_global_device_ids=true, to_apply=%region_41.42 | all-reduce | flops 9228 | bytes 73824 | tf_op jit(solution)/shard_map/psum | solution.py:297
  (415 shorter events, 114.4 us)
Async XLA Ops:
  7.2 48.1 %all-gather.10.cloned.1.call-start = ((), (), s32[]{:S(2)}) async-start(), calls=%async_computation.9 | async-start | bytes 1880064 | tf_op jit(solution)/shard_map/all_gather | solution.py:138
  8.9 74.1 %all-gather.8.cloned.1.call-start = ((), (), s32[]{:S(2)}) async-start(), calls=%async_computation.8 | async-start | bytes 2359296 | tf_op jit(solution)/shard_map/all_gather | solution.py:143
  9.6 236.2 %reduce-scatter.9.cloned.1.call-start = ((), (), s32[]{:S(2)}) async-start(), calls=%async_computation.10 | async-start | bytes 4718592 | tf_op jit(solution)/shard_map/reduce_scatter | solution.py:170
  131.9 9.0 copy-start.97
  185.8 9.0 copy-start.97
  202.4 88.7 %all-gather.14.cloned.1.call-start = ((), (), s32[]{:S(2)}) async-start(), calls=%async_computation.12 | async-start | bytes 2506752 | tf_op jit(solution)/shard_map/all_gather | solution.py:140
  202.4 14.3 %copy-start.31 = (s32[2,2,2,256,52]{3,2,4,1,0:T(2,128)S(1)}, s32[2,2,2,256,52]{3,2,4,1,0:T(2,128)}, u32[]{:S(2)}) copy-start(s32[2,2,2,256,52]{3,2,4,1,0:T(2,128)} %param.30) | copy-start | bytes 1277956
  204.2 132.1 %all-gather.12.cloned.1.call-start = ((), (), s32[]{:S(2)}) async-start(), calls=%async_computation.11 | async-start | bytes 4718592 | tf_op jit(solution)/shard_map/all_gather | solution.py:179
  216.7 216.2 %copy-start.50 = (s32[780]{0:T(1024)}, s32[780]{0:T(1024)S(1)}, u32[]{:S(2)}) copy-start(s32[780]{0:T(1024)S(1)} %shift_right_arithmetic.92) | copy-start | bytes 9364
  220.5 25.4 %copy-start.72 = (f32[768]{0:T(1024)S(1)}, f32[768]{0:T(1024)}, u32[]{:S(2)}) copy-start(f32[768]{0:T(1024)} %get-tuple-element.176) | copy-start | bytes 9220
  224.6 24.2 %copy-start.12 = (s32[2,2,256,768]{3,2,1,0:T(8,128)}, s32[2,2,256,768]{3,2,1,0:T(8,128)S(1)}, u32[]{:S(2)}) copy-start(s32[2,2,256,768]{3,2,1,0:T(8,128)S(1)} %copy.202) | copy-start | bytes 9437188
  224.6 208.3 %copy-start.52 = (f32[768]{0:T(1024)}, f32[768]{0:T(1024)S(1)}, u32[]{:S(2)}) copy-start(f32[768]{0:T(1024)S(1)} %get-tuple-element.181) | copy-start | bytes 9220
  224.6 213.6 %copy-start.40 = (f32[768]{0:T(1024)}, f32[768]{0:T(1024)S(1)}, u32[]{:S(2)}) copy-start(f32[768]{0:T(1024)S(1)} %get-tuple-element.180) | copy-start | bytes 9220
  248.8 184.1 %copy-start.45 = (f32[2,2,256]{2,1,0:T(2,128)}, f32[2,2,256]{2,1,0:T(2,128)S(1)}, u32[]{:S(2)}) copy-start(f32[2,2,256]{2,1,0:T(2,128)S(1)} %broadcast_multiply_fusion.3) | copy-start | bytes 12292
  249.4 183.6 %copy-start.54 = (f32[2,2,256]{2,1,0:T(2,128)}, f32[2,2,256]{2,1,0:T(2,128)S(1)}, u32[]{:S(2)}) copy-start(f32[2,2,256]{2,1,0:T(2,128)S(1)} %fusion.71) | copy-start | bytes 12292
  252.2 129.3 %all-gather.16.cloned.1.call-start = ((), (), s32[]{:S(2)}) async-start(), calls=%async_computation.13 | async-start | bytes 2506752 | tf_op jit(solution)/shard_map/all_gather | solution.py:141
  253.0 179.9 %reduce-scatter.11.cloned.1.call-start = ((), (), s32[]{:S(2)}) async-start(), calls=%async_computation.14 | async-start | bytes 4718592 | tf_op jit(solution)/shard_map/reduce_scatter | solution.py:189
  253.1 118.0 %copy-start.86 = (f32[1536]{0:T(1024)}, f32[1536]{0:T(1024)S(1)}, u32[]{:S(2)}) copy-start(f32[1536]{0:T(1024)S(1)} %dynamic_slice.48) | copy-start | bytes 18436
  390.6 185.4 %all-gather.18.cloned.1.call-start = ((), (), s32[]{:S(2)}) async-start(), calls=%async_computation.15 | async-start | bytes 4718592 | tf_op jit(solution)/shard_map/all_gather | solution.py:208
  392.8 40.1 %copy-start.75 = (f32[768]{0:T(1024)S(1)}, f32[768]{0:T(1024)}, u32[]{:S(2)}) copy-start(f32[768]{0:T(1024)} %get-tuple-element.174) | copy-start | bytes 9220
  437.6 77.0 %copy-start.47 = (f32[2,2,256]{2,1,0:T(2,128)}, f32[2,2,256]{2,1,0:T(2,128)S(1)}, u32[]{:S(2)}) copy-start(f32[2,2,256]{2,1,0:T(2,128)S(1)} %fusion.72) | copy-start | bytes 12292
  532.1 44.0 %copy-start.87 = (f32[1536]{0:T(1024)S(1)}, f32[1536]{0:T(1024)}, u32[]{:S(2)}) copy-start(f32[1536]{0:T(1024)} %copy-done.86) | copy-start | bytes 18436
  535.1 108.6 %reduce-scatter.13.cloned.1.call-start = ((), (), s32[]{:S(2)}) async-start(), calls=%async_computation.16 | async-start | bytes 4718592 | tf_op jit(solution)/shard_map/reduce_scatter | solution.py:215
  576.0 17.6 %copy-start.95 = (bf16[768,1536]{1,0:T(8,128)(2,1)S(1)}, bf16[768,1536]{1,0:T(8,128)(2,1)}, u32[]{:S(2)}) copy-start(bf16[768,1536]{1,0:T(8,128)(2,1)} %all-gather.14.cloned.1.call-done) | copy-start | bytes 7077892
  600.1 43.6 %copy-start.42 = (f32[768]{0:T(1024)S(1)}, f32[768]{0:T(1024)}, u32[]{:S(2)}) copy-start(f32[768]{0:T(1024)} %copy-done.40) | copy-start | bytes 9220
  600.1 43.6 %copy-start.46 = (f32[2,2,256]{2,1,0:T(2,128)S(1)}, f32[2,2,256]{2,1,0:T(2,128)}, u32[]{:S(2)}) copy-start(f32[2,2,256]{2,1,0:T(2,128)} %copy-done.45) | copy-start | bytes 12292
  600.1 43.6 %copy-start.49 = (f32[2,2,256]{2,1,0:T(2,128)S(1)}, f32[2,2,256]{2,1,0:T(2,128)}, u32[]{:S(2)}) copy-start(f32[2,2,256]{2,1,0:T(2,128)} %copy-done.47) | copy-start | bytes 12292
  600.2 43.6 %copy-start.53 = (f32[768]{0:T(1024)S(1)}, f32[768]{0:T(1024)}, u32[]{:S(2)}) copy-start(f32[768]{0:T(1024)} %copy-done.52) | copy-start | bytes 9220
  600.2 43.6 %copy-start.55 = (f32[2,2,256]{2,1,0:T(2,128)S(1)}, f32[2,2,256]{2,1,0:T(2,128)}, u32[]{:S(2)}) copy-start(f32[2,2,256]{2,1,0:T(2,128)} %copy-done.54) | copy-start | bytes 12292
  600.2 48.5 %copy-start.66 = (f32[2,2,256]{2,1,0:T(2,128)S(1)}, f32[2,2,256]{2,1,0:T(2,128)}, u32[]{:S(2)}) copy-start(f32[2,2,256]{2,1,0:T(2,128)} %copy-done.65) | copy-start | bytes 12292
  600.2 99.5 %all-gather.20.cloned.1.call-start = ((), (), s32[]{:S(2)}) async-start(), calls=%async_computation.17 | async-start | bytes 4718592 | tf_op jit(solution)/shard_map/all_gather | solution.py:220
  654.6 172.5 %reduce-scatter.21.cloned.1.call-start = ((), (), s32[]{:S(2)}) async-start(), calls=%async_computation.21 | async-start | bytes 5013504 | tf_op jit(solution)/shard_map/reduce_scatter | solution.py:237
  664.3 193.7 %reduce-scatter.23.cloned.1.call-start = ((), (), s32[]{:S(2)}) async-start(), calls=%async_computation.22 | async-start | bytes 5013504 | tf_op jit(solution)/shard_map/reduce_scatter | solution.py:238
  676.0 23.7 %copy-start.30 = (bf16[384,768]{0,1:T(8,128)(2,1)S(1)}, bf16[384,768]{0,1:T(8,128)(2,1)}, u32[]{:S(2)}) copy-start(bf16[384,768]{0,1:T(8,128)(2,1)} %all_gather.29) | copy-start | bytes 1769476
  676.0 243.1 %reduce-scatter.19.cloned.1.call-start = ((), (), s32[]{:S(2)}) async-start(), calls=%async_computation.20 | async-start | bytes 1253376 | tf_op jit(solution)/shard_map/reduce_scatter | solution.py:236
  712.3 278.1 %reduce-scatter.17.cloned.1.call-start = ((), (), s32[]{:S(2)}) async-start(), calls=%async_computation.19 | async-start | bytes 3760128 | tf_op jit(solution)/shard_map/reduce_scatter | solution.py:235
  723.0 12.6 %copy-start.10 = (bf16[2,512,6,64]{1,3,2,0:T(8,128)(2,1)S(1)}, bf16[2,512,6,64]{1,3,2,0:T(8,128)(2,1)}, u32[]{:S(2)}) copy-start(bf16[2,512,6,64]{1,3,2,0:T(8,128)(2,1)} %get-tuple-element.432) | copy-start | bytes 2359300 | tf_op jit(solution)/shard_map/while
  735.6 10.5 slice-start
  735.6 10.5 slice-start.1
  769.4 12.4 %copy-start.10 = (bf16[2,512,6,64]{1,3,2,0:T(8,128)(2,1)S(1)}, bf16[2,512,6,64]{1,3,2,0:T(8,128)(2,1)}, u32[]{:S(2)}) copy-start(bf16[2,512,6,64]{1,3,2,0:T(8,128)(2,1)} %get-tuple-element.432) | copy-start | bytes 2359300 | tf_op jit(solution)/shard_map/while
  781.8 10.7 slice-start
  781.8 10.7 slice-start.1
  817.0 201.2 %reduce-scatter.15.cloned.1.call-start = ((), (), s32[]{:S(2)}) async-start(), calls=%async_computation.18 | async-start | bytes 2359296 | tf_op jit(solution)/shard_map/reduce_scatter | solution.py:241
  823.6 34.4 %copy-start.21 = (f32[1536,48]{0,1:T(8,128)S(1)}, f32[1536,48]{0,1:T(8,128)}, u32[]{:S(2)}) copy-start(f32[1536,48]{0,1:T(8,128)} %param.40) | copy-start | bytes 884740
  823.7 95.5 %copy-start.29 = (f32[384,48]{0,1:T(8,128)S(1)}, f32[384,48]{0,1:T(8,128)}, u32[]{:S(2)}) copy-start(f32[384,48]{0,1:T(8,128)} %param.34) | copy-start | bytes 221188
  827.1 163.3 %copy-start.22 = (f32[48,3,384]{2,0,1:T(8,128)S(1)}, f32[48,3,384]{2,0,1:T(8,128)}, u32[]{:S(2)}) copy-start(f32[48,3,384]{2,0,1:T(8,128)} %param.31) | copy-start | bytes 663556
  829.9 239.2 %copy-start.23 = (f32[48,1536]{1,0:T(8,128)}, f32[48,1536]{1,0:T(8,128)S(1)}, u32[]{:S(2)}) copy-start(f32[48,1536]{1,0:T(8,128)S(1)} %get-tuple-element.232) | copy-start | bytes 884740
  861.2 160.0 %copy-start.71 = (f32[2,768]{1,0:T(2,128)S(1)}, f32[2,768]{1,0:T(2,128)}, u32[]{:S(2)}) copy-start(f32[2,768]{1,0:T(2,128)} %pad_maximum_fusion.1) | copy-start | bytes 18436
  861.2 202.6 %copy-start.59 = (f32[3072]{0:T(1024)S(1)}, f32[3072]{0:T(1024)}, u32[]{:S(2)}) copy-start(f32[3072]{0:T(1024)} %param.49) | copy-start | bytes 36868
  861.2 202.6 %copy-start.81 = (f32[3072]{0:T(1024)S(1)}, f32[3072]{0:T(1024)}, u32[]{:S(2)}) copy-start(f32[3072]{0:T(1024)} %param.50) | copy-start | bytes 36868
  861.2 202.6 %copy-start.82 = (f32[3072]{0:T(1024)S(1)}, f32[3072]{0:T(1024)}, u32[]{:S(2)}) copy-start(f32[3072]{0:T(1024)} %param.51) | copy-start | bytes 36868
  861.2 204.7 %copy-start.61 = (f32[2,768]{1,0:T(2,128)S(1)}, f32[2,768]{1,0:T(2,128)}, u32[]{:S(2)}) copy-start(f32[2,768]{1,0:T(2,128)} %param.43) | copy-start | bytes 18436
  861.2 204.7 %copy-start.88 = (f32[2,768]{1,0:T(2,128)S(1)}, f32[2,768]{1,0:T(2,128)}, u32[]{:S(2)}) copy-start(f32[2,768]{1,0:T(2,128)} %param.44) | copy-start | bytes 18436
  861.3 204.7 %copy-start.89 = (f32[2,768]{1,0:T(2,128)S(1)}, f32[2,768]{1,0:T(2,128)}, u32[]{:S(2)}) copy-start(f32[2,768]{1,0:T(2,128)} %param.45) | copy-start | bytes 18436
  861.3 206.1 %copy-start.44 = (f32[6,768]{1,0:T(8,128)S(1)}, f32[6,768]{1,0:T(8,128)}, u32[]{:S(2)}) copy-start(f32[6,768]{1,0:T(8,128)} %param.46) | copy-start | bytes 55300
  861.3 206.1 %copy-start.69 = (f32[6,768]{1,0:T(8,128)S(1)}, f32[6,768]{1,0:T(8,128)}, u32[]{:S(2)}) copy-start(f32[6,768]{1,0:T(8,128)} %param.47) | copy-start | bytes 55300
  861.3 206.1 %copy-start.70 = (f32[6,768]{1,0:T(8,128)S(1)}, f32[6,768]{1,0:T(8,128)}, u32[]{:S(2)}) copy-start(f32[6,768]{1,0:T(8,128)} %param.48) | copy-start | bytes 55300
  920.8 147.6 %copy-start.32 = (f32[384,48]{0,1:T(8,128)}, f32[384,48]{0,1:T(8,128)S(1)}, u32[]{:S(2)}) copy-start(f32[384,48]{0,1:T(8,128)S(1)} %get-tuple-element.234) | copy-start | bytes 221188
  920.8 147.6 %copy-start.33 = (f32[384,48]{0,1:T(8,128)}, f32[384,48]{0,1:T(8,128)S(1)}, u32[]{:S(2)}) copy-start(f32[384,48]{0,1:T(8,128)S(1)} %get-tuple-element.235) | copy-start | bytes 221188
  920.8 148.3 %copy-start.24 = (f32[48,1536]{1,0:T(8,128)S(1)}, f32[48,1536]{1,0:T(8,128)}, u32[]{:S(2)}) copy-start(f32[48,1536]{1,0:T(8,128)} %get-tuple-element.233) | copy-start | bytes 884740
  991.9 78.1 %copy-start.27 = (f32[48,3,384]{2,0,1:T(8,128)}, f32[48,3,384]{2,0,1:T(8,128)S(1)}, u32[]{:S(2)}) copy-start(f32[48,3,384]{2,0,1:T(8,128)S(1)} %get-tuple-element.236) | copy-start | bytes 663556
  991.9 78.1 %copy-start.28 = (f32[48,3,384]{2,0,1:T(8,128)}, f32[48,3,384]{2,0,1:T(8,128)S(1)}, u32[]{:S(2)}) copy-start(f32[48,3,384]{2,0,1:T(8,128)S(1)} %get-tuple-element.237) | copy-start | bytes 663556
  1018.2 51.8 %copy-start.25 = (f32[1536,48]{0,1:T(8,128)S(1)}, f32[1536,48]{0,1:T(8,128)}, u32[]{:S(2)}) copy-start(f32[1536,48]{0,1:T(8,128)} %get-tuple-element.230) | copy-start | bytes 884740
  1018.2 51.8 %copy-start.26 = (f32[1536,48]{0,1:T(8,128)S(1)}, f32[1536,48]{0,1:T(8,128)}, u32[]{:S(2)}) copy-start(f32[1536,48]{0,1:T(8,128)} %get-tuple-element.231) | copy-start | bytes 884740
  (71 other events, 268.1 us)
Sparse Core Ops, SparseCore 0:
  10.9 44.3 all-gather.9
  56.8 26.1 all-gather.7
  202.5 43.3 reduce-scatter.8
  248.8 42.2 all-gather.13
  292.5 43.6 all-gather.11
  339.3 42.2 all-gather.15
  390.8 42.1 reduce-scatter.10
  535.2 40.7 all-gather.17
  600.3 43.3 reduce-scatter.12
  654.7 44.9 all-gather.19
  704.1 75.5 reduce-scatter.20
  783.4 74.5 reduce-scatter.22
  862.1 57.0 reduce-scatter.18
  923.4 67.0 reduce-scatter.16
  993.2 24.9 reduce-scatter.14
where the time goes:
time: 1090 us; the launch traced here: 1080 us
  waiting for transfers between devices  474 us (43%)
  matrix products  190 us (17%)
  local copies, waits for them, and re-layouts  159 us (15%)
  blocking collectives  141 us (13%)
  other arithmetic  84 us (8%)
  between operations  20.7 us (2%)
  starting transfers between devices  11.5 us (1%)
    all_gather x1, blocking collectives, shards(): lax.all_gather(pooled_part, ('dp', 'tensor'), axis=1, tiled=True)  74 us
    reduce_scatter x1, waiting for transfers between devices, shards(): lax.psum_scatter(grad_attn_weight, 'dp', scatter_dimension=0, tiled=True)  69.6 us
    dot_general x8, matrix products, contract(): lax.dot_general(left_side, right_side, (((left_dim,), (right_dim,)), ((),...  58.3 us
    reduce_scatter x1, waiting for transfers between devices, shards(): lax.psum_scatter(grad_out, 'dp', scatter_dimension=1, tiled=True)  56.9 us
    while x62, local copies, waits for them, and re-layouts  47.6 us
    all_gather x1, waiting for transfers between devices, shards(): lax.all_gather(normed.astype(jnp.bfloat16), 'tensor', axis=2, tiled=True)  45.2 us
    reduce_scatter x1, waiting for transfers between devices, shards(): lax.psum_scatter(normed_back.astype(jnp.bfloat16), 'tensor', scatter_dime...  43.4 us
    all_gather x1, waiting for transfers between devices, shards(): grad_ffn_full = lax.all_gather(grad_ffn, 'tensor', axis=2, tiled=True)  40.5 us
  transfers between devices with their start and end apart: 15, of which 14 were waited for; matrix products, arithmetic and copies ran while one was open for 20% of the time, Pallas kernels for 0%

commit v1 on v0

--- a/solution.py
+++ b/solution.py
@@ -2,6 +2,7 @@
 import jax.numpy as jnp
 from jax import lax
 from jax.sharding import PartitionSpec as P
+from jax.lax import psum
 
 HD = 64
 STEP = 10
@@ -294,8 +295,8 @@
             ),
         ]
     )
-    summed_squares, gain_total, shift_total, hidden_total = lax.psum(
-        (squares, gain_grads, shift_grads, hidden_grads), ("dp", "tensor")
+    summed_squares, gain_total, shift_total, hidden_total = psum(
+        psum((squares, gain_grads, shift_grads, hidden_grads), "tensor"), "dp"
     )
     trust_ratio = jnp.sqrt(summed_squares[:6]) / jnp.sqrt(summed_squares[6:])
     new_attn = attn_weight - 0.25 * trust_ratio[0:3][None, :, None] * attn_update

time: 1090 us -> 1120 us (1.028)
  blocking collectives: 141 us -> 168 us
    psum x1 -> x2, blocking collectives: 40.1 us -> 67 us  [the longest x1 59.6 us: shards(): psum(psum((squares, gain_grads, shift_grads, hidden_grads), 'tensor'), 'dp')]
where the time goes in v1:
time: 1120 us; the launch traced here: 1110 us
  waiting for transfers between devices  474 us (42%)
  matrix products  190 us (17%)
  blocking collectives  168 us (15%)
  local copies, waits for them, and re-layouts  159 us (14%)
  other arithmetic  84 us (8%)
  between operations  20.7 us (2%)
  starting transfers between devices  11.5 us (1%)
    all_gather x1, blocking collectives, shards(): lax.all_gather(pooled_part, ('dp', 'tensor'), axis=1, tiled=True)  74.1 us
    reduce_scatter x1, waiting for transfers between devices, shards(): lax.psum_scatter(grad_attn_weight, 'dp', scatter_dimension=0, tiled=True)  69.6 us
    psum x1, blocking collectives, shards(): psum(psum((squares, gain_grads, shift_grads, hidden_grads), 'tensor'), 'dp')  59.6 us
    dot_general x8, matrix products, contract(): lax.dot_general(left_side, right_side, (((left_dim,), (right_dim,)), ((),...  58.3 us
    reduce_scatter x1, waiting for transfers between devices, shards(): lax.psum_scatter(grad_out, 'dp', scatter_dimension=1, tiled=True)  56.9 us
    while x62, local copies, waits for them, and re-layouts  47.6 us
    all_gather x1, waiting for transfers between devices, shards(): lax.all_gather(normed.astype(jnp.bfloat16), 'tensor', axis=2, tiled=True)  45.2 us
    reduce_scatter x1, waiting for transfers between devices, shards(): lax.psum_scatter(normed_back.astype(jnp.bfloat16), 'tensor', scatter_dime...  43.4 us
  transfers between devices with their start and end apart: 15, of which 14 were waited for; matrix products, arithmetic and copies ran while one was open for 20% of the time, Pallas kernels for 0%

profile of v1, /device:TPU:0, one launch (start us, length us, event | category | flops | bytes accessed | tf_op | source)
XLA Modules:
  0.0 1107.4 jit_solution(13222384462289387249)
XLA Ops:
  14.4 27.1 %all_gather.29 = bf16[384,768]{0,1:T(8,128)(2,1)} all-gather(bf16[384,48]{0,1:T(8,128)(2,1)S(1)} %convert_element_type.122), channel_id=1, replica_groups=mesh['dp'=16,'tensor'=2] {'dp'}, dimensions={1}, use_global_device_ids=true | all-gather | bytes 626688 | tf_op jit(solution)/shard_map/all_gather | solution.py:140
  41.6 13.7 %all-gather.10.cloned.1.call-done = bf16[768,3,384]{2,0,1:T(8,128)(2,1)} async-done(((bf16[48,3,384]{2,0,1:T(8,128)(2,1)}), bf16[768,3,384]{2,0,1:T(8,128)(2,1)}) %all-gather.10.cloned.1.call-update) | async-done | bytes 1769488 | tf_op jit(solution)/shard_map/all_gather | solution.py:139
  55.3 3.9 copy.163
  59.1 23.8 %all-gather.8.cloned.1.call-done = bf16[2,512,768]{2,1,0:T(8,128)(2,1)} async-done(((bf16[2,256,768]{2,1,0:T(8,128)(2,1)}), bf16[2,512,768]{2,1,0:T(8,128)(2,1)}) %all-gather.8.cloned.1.call-update) | async-done | bytes 1572880 | tf_op jit(solution)/shard_map/all_gather | solution.py:144
  83.0 4.0 add_convert_fusion.1
  88.1 108.0 %while.22 = (s32[]{:T(128)}, bf16[2,2,512,384]{2,3,1,0:T(8,128)(2,1)}, f32[2,6,512]{2,1,0:T(8,128)}, bf16[2,512,6,64]{1,3,2,0:T(8,128)(2,1)}, s32[2,2,6,512,40]{...) while((s32[]{:T(128)}, ...), condition=%wide.region_3.4_spmd, body=%wide.region_0.3_spmd.sunk | while | flops 632681472 | bytes 140713456 | solution.py:162
  88.4 3.6 shift_right_arithmetic.162
  92.0 6.3 slice.162
  98.3 19.1 %copy.239 = s32[2,6,512,512]{3,2,1,0:T(8,128)} copy(s32[2,6,512,512]{2,0,3,1:T(2,128)} %slice.162) | data formatting | bytes 25165824 | tf_op jit(solution)/shard_map/while
  121.6 3.7 exponential_multiply_fusion.2
  125.3 6.6 copy.240
  131.9 8.9 fusion.134
  142.4 3.6 shift_right_arithmetic.162
  146.0 6.3 slice.162
  152.3 19.1 %copy.239 = s32[2,6,512,512]{3,2,1,0:T(8,128)} copy(s32[2,6,512,512]{2,0,3,1:T(2,128)} %slice.162) | data formatting | bytes 25165824 | tf_op jit(solution)/shard_map/while
  175.6 3.7 exponential_multiply_fusion.2
  179.3 6.6 copy.240
  185.9 8.9 fusion.134
  196.1 6.3 convolution_convert_fusion.3
  204.2 9.9 all-gather.12.cloned.1.call-start
  220.5 4.1 copy.202
  224.7 21.3 %reduce-scatter.9.cloned.1.call-done = bf16[2,2,256,768]{3,2,1,0:T(8,128)(2,1)} async-done(((bf16[2,2,512,768]{3,2,1,0:T(8,128)(2,1)}), bf16[2,2,256,768]{3,2,1,0:T(8,128)(2,1)}) %reduce-scatter.9.cloned.1.call-update) | async-done | bytes 1572880 | tf_op jit(solution)/shard_map/reduce_scatter | solution.py:171
  253.2 37.9 %all-gather.14.cloned.1.call-done = bf16[768,1536]{1,0:T(8,128)(2,1)} async-done(((bf16[48,1536]{1,0:T(8,128)(2,1)}), bf16[768,1536]{1,0:T(8,128)(2,1)}) %all-gather.14.cloned.1.call-update) | async-done | bytes 2359312 | tf_op jit(solution)/shard_map/all_gather | solution.py:141
  291.1 45.2 %all-gather.12.cloned.1.call-done = bf16[2,2,512,768]{3,2,1,0:T(8,128)(2,1)} async-done(((bf16[2,2,256,768]{3,2,1,0:T(8,128)(2,1)}), bf16[2,2,512,768]{3,2,1,0:T(8,128)(2,1)}) %all-gather.12.cloned.1.call-update) | async-done | bytes 3145744 | tf_op jit(solution)/shard_map/all_gather | solution.py:180
  336.3 34.9 %multiply_convert_fusion.6 = (bf16[2048,1536]{1,0:T(8,128)(2,1)}, f32[2048,1536]{1,0:T(8,128)}, f32[2048,1536]{1,0:T(8,128)}) fusion(f32[1536]{0:T(1024)S(1)} %dynamic_slice.48, bf16[2048,768]{1,0:T(8,128)(2,1)} %bitcast.269, bf16[768,1536]{1,0:T(8,128)(2,1)} %all-gather.14.cloned.1.call-done), kind=kOutput, calls=%fused_computation.68 | convolution fusion | flops 5039456256 | bytes 36968448 | tf_op jit(solution)/shard_map/dot_general | solution.py:183
  371.2 10.3 all-gather.16.cloned.1.call-done
  381.6 9.1 convolution_convert_fusion.1
  392.9 3.6 copy.203
  397.0 36.0 %reduce-scatter.11.cloned.1.call-done = bf16[2,2,256,768]{3,2,1,0:T(8,128)(2,1)} async-done(((bf16[2,2,512,768]{3,2,1,0:T(8,128)(2,1)}), bf16[2,2,256,768]{3,2,1,0:T(8,128)(2,1)}) %reduce-scatter.11.cloned.1.call-update) | async-done | bytes 1572880 | tf_op jit(solution)/shard_map/reduce_scatter | solution.py:190
  433.0 4.1 fusion.84
  438.9 74.1 %all_gather.33 = f32[2,64,768]{2,0,1:T(2,128)} all-gather(f32[2,2,768]{2,0,1:T(2,128)S(1)} %copy.168), channel_id=1, replica_groups=mesh['dp'=16,'tensor'=2] {'dp','tensor'}, dimensions={1}, use_global_device_ids=true | all-gather | bytes 405504 | tf_op jit(solution)/shard_map/all_gather | solution.py:197
  535.6 40.5 %all-gather.18.cloned.1.call-done = bf16[2,2,512,768]{3,2,1,0:T(8,128)(2,1)} async-done(((bf16[2,2,256,768]{3,2,1,0:T(8,128)(2,1)}), bf16[2,2,512,768]{3,2,1,0:T(8,128)(2,1)}) %all-gather.18.cloned.1.call-update) | async-done | bytes 3145744 | tf_op jit(solution)/shard_map/all_gather | solution.py:209
  576.1 17.6 %convert_reduce_fusion = (f32[1536]{0:T(1024)}, bf16[2048,1536]{1,0:T(8,128)(2,1)S(1)}) fusion(f32[2048,1536]{1,0:T(8,128)} %get-tuple-element.247, bf16[2048,768]{1,0:T(8,128)(2,1)} %bitcast.271, bf16[1536,768]{0,1:T(8,128)(2,1)} %all-gather.16.cloned.1.call-done, f32[2048,1536]{1,0:T(8,128)} %get-tuple-element.274, f32[1536]{0:T(1024)S(1)} %copy-done.87), kind=kOutput, calls=%fused_computation.66 | convolution fusion | flops 4885314048 | bytes 36974592 | tf_op jit(solution)/shard_map/dot_general | solution.py:36
  593.7 6.5 convolution_convert_fusion
  600.3 43.4 %reduce-scatter.13.cloned.1.call-done = bf16[2,2,256,768]{3,2,1,0:T(8,128)(2,1)} async-done(((bf16[2,2,512,768]{3,2,1,0:T(8,128)(2,1)}), bf16[2,2,256,768]{3,2,1,0:T(8,128)(2,1)}) %reduce-scatter.13.cloned.1.call-update) | async-done | bytes 1572880 | tf_op jit(solution)/shard_map/reduce_scatter | solution.py:216
  643.8 5.0 multiply_reduce_fusion.3
  654.7 9.6 fusion.92
  666.5 9.5 fusion.93
  676.1 23.7 %all-gather.20.cloned.1.call-done = bf16[2,2,512,768]{3,2,1,0:T(8,128)(2,1)} async-done(((bf16[2,2,256,768]{3,2,1,0:T(8,128)(2,1)}), bf16[2,2,512,768]{3,2,1,0:T(8,128)(2,1)}) %all-gather.20.cloned.1.call-update) | async-done | bytes 3145744 | tf_op jit(solution)/shard_map/all_gather | solution.py:221
  699.8 3.7 convolution_convert_fusion.2
  707.9 4.5 convolution_bitcast_fusion
  712.7 93.9 %while.23 = (s32[]{:T(128)}, bf16[2,512,3,6,64]{1,4,3,2,0:T(8,128)(2,1)}, bf16[2,512,6,64]{1,3,2,0:T(8,128)(2,1)S(1)}, bf16[2,512,6,64]{1,3,2,0:T(8,128)(2,1)}, ...) while((s32[]{:T(128)}, ...), condition=%wide.region_26.27_spmd, body=%wide.region_23.26_spmd.sunk | while | flops 1462367232 | bytes 228946432 | solution.py:229
  713.0 3.6 shift_right_arithmetic.169
  716.6 6.3 slice.164
  723.1 12.5 %fusion.142 = f32[6,512,512]{1,2,0:T(8,128)} fusion(s32[2,6,512,512]{2,0,3,1:T(2,128)} %slice.164, s32[512]{0:T(512)S(1)} %slice.165, bf16[2,2,512,6,64]{2,4,1,3,0:T(8,128)(2,1)} %get-tuple-element.439, s32[]{:T(128)S(6)} %copy.259, bf16[2,512,6,64]{1,3,2,0:T(8,128)(2,1)} %get-tuple-element.438), kind=kOutput, calls=%fused_computation.27.clone.1 | convolution fusion | flops 419954688 | bytes 20057088 | tf_op jit(solution)/shard_map/while/body/eval_jaxpr/vqhd,khd->vhqk/dot_general | solution.py:69
  735.7 4.8 multiply_reduce_fusion.25
  740.5 5.6 multiply_convert_fusion.18
  747.4 6.1 fusion.143
  759.5 3.6 shift_right_arithmetic.169
  763.1 6.3 slice.164
  769.5 12.4 %fusion.142 = f32[6,512,512]{1,2,0:T(8,128)} fusion(s32[2,6,512,512]{2,0,3,1:T(2,128)} %slice.164, s32[512]{0:T(512)S(1)} %slice.165, bf16[2,2,512,6,64]{2,4,1,3,0:T(8,128)(2,1)} %get-tuple-element.439, s32[]{:T(128)S(6)} %copy.259, bf16[2,512,6,64]{1,3,2,0:T(8,128)(2,1)} %get-tuple-element.438), kind=kOutput, calls=%fused_computation.27.clone.1 | convolution fusion | flops 419954688 | bytes 20057088 | tf_op jit(solution)/shard_map/while/body/eval_jaxpr/vqhd,khd->vhqk/dot_general | solution.py:69
  782.0 4.8 multiply_reduce_fusion.25
  786.8 5.9 multiply_convert_fusion.18
  794.1 6.3 fusion.143
  800.5 3.4 fusion.144
  806.6 4.1 copy.178
  818.8 5.0 convolution_convert_fusion.4
  830.0 28.1 %reduce-scatter.23.cloned.1.call-done = f32[1536,48]{0,1:T(8,128)} async-done(((f32[1536,768]{0,1:T(8,128)}), f32[1536,48]{0,1:T(8,128)}) %reduce-scatter.23.cloned.1.call-update) | async-done | bytes 294928 | tf_op jit(solution)/shard_map/reduce_scatter | solution.py:239
  862.3 56.9 %reduce-scatter.19.cloned.1.call-done = f32[384,48]{0,1:T(8,128)} async-done(((f32[384,768]{0,1:T(8,128)}), f32[384,48]{0,1:T(8,128)}) %reduce-scatter.19.cloned.1.call-update) | async-done | bytes 73744 | tf_op jit(solution)/shard_map/reduce_scatter | solution.py:237
  920.9 69.6 %reduce-scatter.17.cloned.1.call-done = f32[48,3,384]{2,0,1:T(8,128)} async-done(((f32[768,3,384]{2,0,1:T(8,128)}), f32[48,3,384]{2,0,1:T(8,128)}) %reduce-scatter.17.cloned.1.call-update) | async-done | bytes 221200 | tf_op jit(solution)/shard_map/reduce_scatter | solution.py:236
  992.0 4.0 concatenate.8
  995.9 22.4 %reduce-scatter.15.cloned.1.call-done = bf16[2,256,768]{2,1,0:T(8,128)(2,1)} async-done(((bf16[2,512,768]{2,1,0:T(8,128)(2,1)}), bf16[2,256,768]{2,1,0:T(8,128)(2,1)}) %reduce-scatter.15.cloned.1.call-update) | async-done | bytes 786448 | tf_op jit(solution)/shard_map/reduce_scatter | solution.py:242
  1021.3 7.4 all-reduce.3
  1028.7 59.6 %all-reduce.2 = (f32[12]{0:T(128)S(1)}, f32[2,768]{1,0:T(2,128)S(1)}, f32[6,768]{1,0:T(8,128)S(1)}, f32[3072]{0:T(1024)S(1)}) all-reduce(f32[12]{0:T(128)S(1)} %get-tuple-element.216, f32[2,768]{1,0:T(2,128)S(1)} %get-tuple-element.217, f32[6,768]{1,0:T(8,128)S(1)} %get-tuple-element.218, ...), channel_id=1, replica_groups=mesh['dp'=16,'tensor'=2] {'dp'}, use_global_device_ids=true, to_apply=%region_42.43 | all-reduce | flops 9228 | bytes 73824 | tf_op jit(solution)/shard_map/psum | solution.py:298
  (416 shorter events, 117.7 us)
Async XLA Ops:
  7.2 48.1 %all-gather.10.cloned.1.call-start = ((), (), s32[]{:S(2)}) async-start(), calls=%async_computation.9 | async-start | bytes 1880064 | tf_op jit(solution)/shard_map/all_gather | solution.py:139
  8.9 74.1 %all-gather.8.cloned.1.call-start = ((), (), s32[]{:S(2)}) async-start(), calls=%async_computation.8 | async-start | bytes 2359296 | tf_op jit(solution)/shard_map/all_gather | solution.py:144
  9.6 236.3 %reduce-scatter.9.cloned.1.call-start = ((), (), s32[]{:S(2)}) async-start(), calls=%async_computation.10 | async-start | bytes 4718592 | tf_op jit(solution)/shard_map/reduce_scatter | solution.py:171
  131.9 9.0 copy-start.97
  185.9 9.0 copy-start.97
  202.4 88.7 %all-gather.14.cloned.1.call-start = ((), (), s32[]{:S(2)}) async-start(), calls=%async_computation.12 | async-start | bytes 2506752 | tf_op jit(solution)/shard_map/all_gather | solution.py:141
  202.5 14.2 %copy-start.31 = (s32[2,2,2,256,52]{3,2,4,1,0:T(2,128)S(1)}, s32[2,2,2,256,52]{3,2,4,1,0:T(2,128)}, u32[]{:S(2)}) copy-start(s32[2,2,2,256,52]{3,2,4,1,0:T(2,128)} %param.30) | copy-start | bytes 1277956
  204.2 132.1 %all-gather.12.cloned.1.call-start = ((), (), s32[]{:S(2)}) async-start(), calls=%async_computation.11 | async-start | bytes 4718592 | tf_op jit(solution)/shard_map/all_gather | solution.py:180
  216.7 216.2 %copy-start.50 = (s32[780]{0:T(1024)}, s32[780]{0:T(1024)S(1)}, u32[]{:S(2)}) copy-start(s32[780]{0:T(1024)S(1)} %shift_right_arithmetic.92) | copy-start | bytes 9364
  220.5 25.4 %copy-start.72 = (f32[768]{0:T(1024)S(1)}, f32[768]{0:T(1024)}, u32[]{:S(2)}) copy-start(f32[768]{0:T(1024)} %get-tuple-element.176) | copy-start | bytes 9220
  224.6 24.2 %copy-start.12 = (s32[2,2,256,768]{3,2,1,0:T(8,128)}, s32[2,2,256,768]{3,2,1,0:T(8,128)S(1)}, u32[]{:S(2)}) copy-start(s32[2,2,256,768]{3,2,1,0:T(8,128)S(1)} %copy.202) | copy-start | bytes 9437188
  224.6 208.3 %copy-start.52 = (f32[768]{0:T(1024)}, f32[768]{0:T(1024)S(1)}, u32[]{:S(2)}) copy-start(f32[768]{0:T(1024)S(1)} %get-tuple-element.181) | copy-start | bytes 9220
  224.7 213.6 %copy-start.40 = (f32[768]{0:T(1024)}, f32[768]{0:T(1024)S(1)}, u32[]{:S(2)}) copy-start(f32[768]{0:T(1024)S(1)} %get-tuple-element.180) | copy-start | bytes 9220
  248.9 184.1 %copy-start.45 = (f32[2,2,256]{2,1,0:T(2,128)}, f32[2,2,256]{2,1,0:T(2,128)S(1)}, u32[]{:S(2)}) copy-start(f32[2,2,256]{2,1,0:T(2,128)S(1)} %broadcast_multiply_fusion.3) | copy-start | bytes 12292
  249.4 183.5 %copy-start.54 = (f32[2,2,256]{2,1,0:T(2,128)}, f32[2,2,256]{2,1,0:T(2,128)S(1)}, u32[]{:S(2)}) copy-start(f32[2,2,256]{2,1,0:T(2,128)S(1)} %fusion.71) | copy-start | bytes 12292
  252.3 129.3 %all-gather.16.cloned.1.call-start = ((), (), s32[]{:S(2)}) async-start(), calls=%async_computation.13 | async-start | bytes 2506752 | tf_op jit(solution)/shard_map/all_gather | solution.py:142
  253.1 179.9 %reduce-scatter.11.cloned.1.call-start = ((), (), s32[]{:S(2)}) async-start(), calls=%async_computation.14 | async-start | bytes 4718592 | tf_op jit(solution)/shard_map/reduce_scatter | solution.py:190
  253.2 118.0 %copy-start.86 = (f32[1536]{0:T(1024)}, f32[1536]{0:T(1024)S(1)}, u32[]{:S(2)}) copy-start(f32[1536]{0:T(1024)S(1)} %dynamic_slice.48) | copy-start | bytes 18436
  390.7 185.4 %all-gather.18.cloned.1.call-start = ((), (), s32[]{:S(2)}) async-start(), calls=%async_computation.15 | async-start | bytes 4718592 | tf_op jit(solution)/shard_map/all_gather | solution.py:209
  392.9 40.1 %copy-start.75 = (f32[768]{0:T(1024)S(1)}, f32[768]{0:T(1024)}, u32[]{:S(2)}) copy-start(f32[768]{0:T(1024)} %get-tuple-element.174) | copy-start | bytes 9220
  437.7 77.1 %copy-start.47 = (f32[2,2,256]{2,1,0:T(2,128)}, f32[2,2,256]{2,1,0:T(2,128)S(1)}, u32[]{:S(2)}) copy-start(f32[2,2,256]{2,1,0:T(2,128)S(1)} %fusion.72) | copy-start | bytes 12292
  532.1 44.0 %copy-start.87 = (f32[1536]{0:T(1024)S(1)}, f32[1536]{0:T(1024)}, u32[]{:S(2)}) copy-start(f32[1536]{0:T(1024)} %copy-done.86) | copy-start | bytes 18436
  535.1 108.6 %reduce-scatter.13.cloned.1.call-start = ((), (), s32[]{:S(2)}) async-start(), calls=%async_computation.16 | async-start | bytes 4718592 | tf_op jit(solution)/shard_map/reduce_scatter | solution.py:216
  576.1 17.6 %copy-start.95 = (bf16[768,1536]{1,0:T(8,128)(2,1)S(1)}, bf16[768,1536]{1,0:T(8,128)(2,1)}, u32[]{:S(2)}) copy-start(bf16[768,1536]{1,0:T(8,128)(2,1)} %all-gather.14.cloned.1.call-done) | copy-start | bytes 7077892
  600.2 43.6 %copy-start.42 = (f32[768]{0:T(1024)S(1)}, f32[768]{0:T(1024)}, u32[]{:S(2)}) copy-start(f32[768]{0:T(1024)} %copy-done.40) | copy-start | bytes 9220
  600.2 43.6 %copy-start.46 = (f32[2,2,256]{2,1,0:T(2,128)S(1)}, f32[2,2,256]{2,1,0:T(2,128)}, u32[]{:S(2)}) copy-start(f32[2,2,256]{2,1,0:T(2,128)} %copy-done.45) | copy-start | bytes 12292
  600.2 43.6 %copy-start.49 = (f32[2,2,256]{2,1,0:T(2,128)S(1)}, f32[2,2,256]{2,1,0:T(2,128)}, u32[]{:S(2)}) copy-start(f32[2,2,256]{2,1,0:T(2,128)} %copy-done.47) | copy-start | bytes 12292
  600.2 43.6 %copy-start.53 = (f32[768]{0:T(1024)S(1)}, f32[768]{0:T(1024)}, u32[]{:S(2)}) copy-start(f32[768]{0:T(1024)} %copy-done.52) | copy-start | bytes 9220
  600.2 43.6 %copy-start.55 = (f32[2,2,256]{2,1,0:T(2,128)S(1)}, f32[2,2,256]{2,1,0:T(2,128)}, u32[]{:S(2)}) copy-start(f32[2,2,256]{2,1,0:T(2,128)} %copy-done.54) | copy-start | bytes 12292
  600.2 48.5 %copy-start.66 = (f32[2,2,256]{2,1,0:T(2,128)S(1)}, f32[2,2,256]{2,1,0:T(2,128)}, u32[]{:S(2)}) copy-start(f32[2,2,256]{2,1,0:T(2,128)} %copy-done.65) | copy-start | bytes 12292
  600.3 99.5 %all-gather.20.cloned.1.call-start = ((), (), s32[]{:S(2)}) async-start(), calls=%async_computation.17 | async-start | bytes 4718592 | tf_op jit(solution)/shard_map/all_gather | solution.py:221
  654.7 172.6 %reduce-scatter.21.cloned.1.call-start = ((), (), s32[]{:S(2)}) async-start(), calls=%async_computation.21 | async-start | bytes 5013504 | tf_op jit(solution)/shard_map/reduce_scatter | solution.py:238
  664.3 193.8 %reduce-scatter.23.cloned.1.call-start = ((), (), s32[]{:S(2)}) async-start(), calls=%async_computation.22 | async-start | bytes 5013504 | tf_op jit(solution)/shard_map/reduce_scatter | solution.py:239
  676.0 23.8 %copy-start.30 = (bf16[384,768]{0,1:T(8,128)(2,1)S(1)}, bf16[384,768]{0,1:T(8,128)(2,1)}, u32[]{:S(2)}) copy-start(bf16[384,768]{0,1:T(8,128)(2,1)} %all_gather.29) | copy-start | bytes 1769476
  676.0 243.2 %reduce-scatter.19.cloned.1.call-start = ((), (), s32[]{:S(2)}) async-start(), calls=%async_computation.20 | async-start | bytes 1253376 | tf_op jit(solution)/shard_map/reduce_scatter | solution.py:237
  712.4 278.1 %reduce-scatter.17.cloned.1.call-start = ((), (), s32[]{:S(2)}) async-start(), calls=%async_computation.19 | async-start | bytes 3760128 | tf_op jit(solution)/shard_map/reduce_scatter | solution.py:236
  723.1 12.5 %copy-start.10 = (bf16[2,512,6,64]{1,3,2,0:T(8,128)(2,1)S(1)}, bf16[2,512,6,64]{1,3,2,0:T(8,128)(2,1)}, u32[]{:S(2)}) copy-start(bf16[2,512,6,64]{1,3,2,0:T(8,128)(2,1)} %get-tuple-element.436) | copy-start | bytes 2359300 | tf_op jit(solution)/shard_map/while
  735.6 10.5 slice-start
  735.6 10.5 slice-start.1
  769.5 12.4 %copy-start.10 = (bf16[2,512,6,64]{1,3,2,0:T(8,128)(2,1)S(1)}, bf16[2,512,6,64]{1,3,2,0:T(8,128)(2,1)}, u32[]{:S(2)}) copy-start(bf16[2,512,6,64]{1,3,2,0:T(8,128)(2,1)} %get-tuple-element.436) | copy-start | bytes 2359300 | tf_op jit(solution)/shard_map/while
  781.9 10.7 slice-start
  781.9 10.7 slice-start.1
  817.1 201.2 %reduce-scatter.15.cloned.1.call-start = ((), (), s32[]{:S(2)}) async-start(), calls=%async_computation.18 | async-start | bytes 2359296 | tf_op jit(solution)/shard_map/reduce_scatter | solution.py:242
  823.8 34.3 %copy-start.21 = (f32[1536,48]{0,1:T(8,128)S(1)}, f32[1536,48]{0,1:T(8,128)}, u32[]{:S(2)}) copy-start(f32[1536,48]{0,1:T(8,128)} %param.40) | copy-start | bytes 884740
  823.8 95.4 %copy-start.29 = (f32[384,48]{0,1:T(8,128)S(1)}, f32[384,48]{0,1:T(8,128)}, u32[]{:S(2)}) copy-start(f32[384,48]{0,1:T(8,128)} %param.34) | copy-start | bytes 221188
  827.3 163.2 %copy-start.22 = (f32[48,3,384]{2,0,1:T(8,128)S(1)}, f32[48,3,384]{2,0,1:T(8,128)}, u32[]{:S(2)}) copy-start(f32[48,3,384]{2,0,1:T(8,128)} %param.31) | copy-start | bytes 663556
  830.0 266.1 %copy-start.23 = (f32[48,1536]{1,0:T(8,128)}, f32[48,1536]{1,0:T(8,128)S(1)}, u32[]{:S(2)}) copy-start(f32[48,1536]{1,0:T(8,128)S(1)} %get-tuple-element.236) | copy-start | bytes 884740
  861.3 160.0 %copy-start.71 = (f32[2,768]{1,0:T(2,128)S(1)}, f32[2,768]{1,0:T(2,128)}, u32[]{:S(2)}) copy-start(f32[2,768]{1,0:T(2,128)} %pad_maximum_fusion.1) | copy-start | bytes 18436
  861.3 229.6 %copy-start.59 = (f32[3072]{0:T(1024)S(1)}, f32[3072]{0:T(1024)}, u32[]{:S(2)}) copy-start(f32[3072]{0:T(1024)} %param.49) | copy-start | bytes 36868
  861.3 229.6 %copy-start.81 = (f32[3072]{0:T(1024)S(1)}, f32[3072]{0:T(1024)}, u32[]{:S(2)}) copy-start(f32[3072]{0:T(1024)} %param.50) | copy-start | bytes 36868
  861.3 229.6 %copy-start.82 = (f32[3072]{0:T(1024)S(1)}, f32[3072]{0:T(1024)}, u32[]{:S(2)}) copy-start(f32[3072]{0:T(1024)} %param.51) | copy-start | bytes 36868
  861.3 231.7 %copy-start.61 = (f32[2,768]{1,0:T(2,128)S(1)}, f32[2,768]{1,0:T(2,128)}, u32[]{:S(2)}) copy-start(f32[2,768]{1,0:T(2,128)} %param.43) | copy-start | bytes 18436
  861.3 231.7 %copy-start.88 = (f32[2,768]{1,0:T(2,128)S(1)}, f32[2,768]{1,0:T(2,128)}, u32[]{:S(2)}) copy-start(f32[2,768]{1,0:T(2,128)} %param.44) | copy-start | bytes 18436
  861.3 231.7 %copy-start.89 = (f32[2,768]{1,0:T(2,128)S(1)}, f32[2,768]{1,0:T(2,128)}, u32[]{:S(2)}) copy-start(f32[2,768]{1,0:T(2,128)} %param.45) | copy-start | bytes 18436
  861.3 233.1 %copy-start.44 = (f32[6,768]{1,0:T(8,128)S(1)}, f32[6,768]{1,0:T(8,128)}, u32[]{:S(2)}) copy-start(f32[6,768]{1,0:T(8,128)} %param.46) | copy-start | bytes 55300
  861.4 233.1 %copy-start.69 = (f32[6,768]{1,0:T(8,128)S(1)}, f32[6,768]{1,0:T(8,128)}, u32[]{:S(2)}) copy-start(f32[6,768]{1,0:T(8,128)} %param.47) | copy-start | bytes 55300
  861.4 233.1 %copy-start.70 = (f32[6,768]{1,0:T(8,128)S(1)}, f32[6,768]{1,0:T(8,128)}, u32[]{:S(2)}) copy-start(f32[6,768]{1,0:T(8,128)} %param.48) | copy-start | bytes 55300
  920.9 174.6 %copy-start.32 = (f32[384,48]{0,1:T(8,128)}, f32[384,48]{0,1:T(8,128)S(1)}, u32[]{:S(2)}) copy-start(f32[384,48]{0,1:T(8,128)S(1)} %get-tuple-element.238) | copy-start | bytes 221188
  920.9 174.6 %copy-start.33 = (f32[384,48]{0,1:T(8,128)}, f32[384,48]{0,1:T(8,128)S(1)}, u32[]{:S(2)}) copy-start(f32[384,48]{0,1:T(8,128)S(1)} %get-tuple-element.239) | copy-start | bytes 221188
  920.9 175.3 %copy-start.24 = (f32[48,1536]{1,0:T(8,128)S(1)}, f32[48,1536]{1,0:T(8,128)}, u32[]{:S(2)}) copy-start(f32[48,1536]{1,0:T(8,128)} %get-tuple-element.237) | copy-start | bytes 884740
  992.0 105.1 %copy-start.27 = (f32[48,3,384]{2,0,1:T(8,128)}, f32[48,3,384]{2,0,1:T(8,128)S(1)}, u32[]{:S(2)}) copy-start(f32[48,3,384]{2,0,1:T(8,128)S(1)} %get-tuple-element.240) | copy-start | bytes 663556
  992.0 105.1 %copy-start.28 = (f32[48,3,384]{2,0,1:T(8,128)}, f32[48,3,384]{2,0,1:T(8,128)S(1)}, u32[]{:S(2)}) copy-start(f32[48,3,384]{2,0,1:T(8,128)S(1)} %get-tuple-element.241) | copy-start | bytes 663556
  1018.3 78.7 %copy-start.25 = (f32[1536,48]{0,1:T(8,128)S(1)}, f32[1536,48]{0,1:T(8,128)}, u32[]{:S(2)}) copy-start(f32[1536,48]{0,1:T(8,128)} %get-tuple-element.234) | copy-start | bytes 884740
  1018.3 78.7 %copy-start.26 = (f32[1536,48]{0,1:T(8,128)S(1)}, f32[1536,48]{0,1:T(8,128)}, u32[]{:S(2)}) copy-start(f32[1536,48]{0,1:T(8,128)} %get-tuple-element.235) | copy-start | bytes 884740
  (71 other events, 268.1 us)
Sparse Core Ops, SparseCore 0:
  10.9 44.3 all-gather.9
  56.8 26.1 all-gather.7
  202.5 43.3 reduce-scatter.8
  248.9 42.2 all-gather.13
  292.6 43.6 all-gather.11
  339.3 42.2 all-gather.15
  390.8 42.0 reduce-scatter.10
  535.3 40.7 all-gather.17
  600.4 43.3 reduce-scatter.12
  654.8 44.9 all-gather.19
  704.1 75.5 reduce-scatter.20
  783.5 74.5 reduce-scatter.22
  862.1 57.0 reduce-scatter.18
  923.5 66.9 reduce-scatter.16
  993.3 25.0 reduce-scatter.14
